TPU v7x, 256 devices: a whole 4x4x8 slice. The times are simulated.
256 devices in a mesh: rows: 32 (over x, z), vecs: 8 (over y, core).
Axes of the slice: x: 4, y: 4, z: 8, core: 2. Of those that a mesh axis runs over, the one named last changes fastest.
Arguments:
- coords: float32 [3, 8192], P(None, ('rows', 'vecs')), may hold values from 0 to 1
- old_vectors: bfloat16 [8192, 16384], P('rows', 'vecs'), may hold values from -0.078125 to 0.078125
- pivots: int32 [2, 128], replicated, may hold values from 0 to 8191, as said below
- slots: int32 [8192], replicated, may hold values from 0 to 8191, each once
Outputs:
- new_vectors: float32 [8192, 256], P(('rows', 'vecs'))
Inputs may be any that keep to these rules, and one draw needn't show every extreme that they name: `pivots`: all 256 pivot numbers are distinct. `slots`: each window row belongs to exactly one point.
All inputs are finite; a program needn't handle non-finite values.
Results may differ from a plain program's by a relative error of at most 0.0003.
Values may be sent and summed in bfloat16 or wider, within the bound.
A program may use at most 64 MiB of HBM per device.

v0:
```python
import jax
import jax.numpy as jnp
from jax import lax
from jax.sharding import PartitionSpec as P

length_scale = 0.5
noise_shift = 12.0


def matern(points, centers):
    dist_sq = jnp.zeros((points.shape[1], centers.shape[1]), jnp.float32)
    for component in range(3):
        differ = points[component][:, None] - centers[component][None, :]
        dist_sq = dist_sq + differ * differ
    scaled = jnp.sqrt(5.0 * dist_sq) / length_scale
    return (1.0 + scaled + scaled * scaled / 3.0) * jnp.exp(-scaled)


def pick_rows(block_data, wanted, first_row):
    length = block_data.shape[0]
    offset = wanted - first_row
    inside = (offset >= 0) & (offset < length)
    bounded = jnp.clip(offset, 0, length - 1)
    fetched = jnp.take(block_data, bounded, axis=0)
    return jnp.where(inside[:, None], fetched, jnp.zeros((), block_data.dtype))


def shards(coords, old_vectors, pivots, slots):
    row_block = old_vectors.shape[0]
    share = coords.shape[1]
    panels = pivots.shape[0]
    width = pivots.shape[1]
    block_first = lax.axis_index("rows") * row_block
    share_first = block_first + lax.axis_index("vecs") * share
    wanted = jnp.take(slots, pivots.reshape(-1), axis=0)
    my_rows = share_first + jnp.arange(share, dtype=jnp.int32)
    every_point = lax.all_gather(coords, ("rows", "vecs"), axis=1, tiled=True)
    centers = jnp.take(every_point, wanted, axis=1)
    new_panels = []
    for panel in range(panels):
        chosen = wanted[panel * width : (panel + 1) * width]
        old_pivot = (
            lax.psum(pick_rows(old_vectors, chosen, block_first), "rows")
            .astype(jnp.float32)
            .astype(jnp.bfloat16)
        )

        def residual_term(first_row, length, old_pivot=old_pivot):
            return jnp.dot(old_vectors, old_pivot.T, preferred_element_type=jnp.float32)

        summed = lax.psum_scatter(
            residual_term(jnp.int32(0), share * lax.axis_size("vecs")),
            "vecs",
            scatter_dimension=0,
            tiled=True,
        )
        kernel = matern(coords, centers[:, panel * width : (panel + 1) * width])
        kernel = kernel + noise_shift * (my_rows[:, None] == chosen[None, :]).astype(jnp.float32)
        current = kernel - summed
        if panel > 0:
            stacked = new_panels[0]
            earlier = lax.psum(pick_rows(stacked, chosen, share_first), ("rows", "vecs"))
            current = current - jnp.dot(
                stacked,
                earlier.T,
                precision=lax.Precision.HIGHEST,
                preferred_element_type=jnp.float32,
            )
        block = lax.psum(pick_rows(current, chosen, share_first), ("rows", "vecs"))
        factor = jnp.linalg.cholesky(block)
        fresh = jax.scipy.linalg.solve_triangular(factor, current.T, lower=True).T
        new_panels.append(fresh)
    return jnp.concatenate(new_panels, axis=1)


def solution(mesh):
    in_specs = (P(None, ("rows", "vecs")), P("rows", "vecs"), P(), P())
    out_specs = P(("rows", "vecs"), None)
    return jax.shard_map(shards, mesh=mesh, in_specs=in_specs, out_specs=out_specs, check_vma=False)
```

profile of v0, /device:TPU:1, one launch (start us, length us, event | category | flops | bytes accessed | tf_op | source)
XLA Modules:
  0.0 1000.4 jit_solution(14306244718149790146)
XLA Ops:
  6.5 0.8 compare_select_fusion.1
  7.3 2.0 gather_fusion
  9.3 0.7 compare_and_fusion.7
  10.1 0.9 gather_fusion.4
  11.0 0.9 gather_fusion.2
  12.0 1.2 select_select_fusion
  13.2 73.2 %all-gather = f32[256,32,3]{1,2,0:T(4,128)S(1)} all-gather(f32[1,32,3]{1,2,0:T(4,128)S(1)} %bitcast.66), channel_id=1, replica_groups=mesh['rows'=32,'vecs'=8] {'rows','vecs'}, dimensions={0}, use_global_device_ids=true | all-gather | bytes 98688 | tf_op jit(solution)/shard_map/all_gather | solution.py:37
  86.5 3.0 copy.23
  89.5 2.9 gather_fusion.1
  92.4 0.1 select_bitcast_fusion
  92.5 0.3 slice_reduce_fusion.2
  92.8 70.1 %all-reduce.12.cloned.1.call-done = (bf16[128,2048]{1,0:T(8,128)(2,1)}, bf16[128,2048]{1,0:T(8,128)(2,1)}) async-done(((bf16[128,2048]{1,0:T(8,128)(2,1)}, bf16[128,2048]{1,0:T(8,128)(2,1)}), (bf16[128,2048]{1,0:T(8,128)(2,1)}, bf16[128,2048]{1,0:T(8,128)(2,1)})) %all-reduce.12.cloned.1.call-update) | async-done | bytes 1048592 | tf_op jit(solution)/shard_map/psum | solution.py:43
  162.9 1.5 convolution_bitcast_fusion.1
  164.4 0.7 copy.31
  165.3 33.3 %reduce-scatter.7.cloned.1.call-done = f32[32,128]{1,0:T(8,128)} async-done(((f32[256,128]{1,0:T(8,128)}), f32[32,128]{1,0:T(8,128)}) %reduce-scatter.7.cloned.1.call-update) | async-done | bytes 16400 | tf_op jit(solution)/shard_map/reduce_scatter | solution.py:51
  198.5 0.8 add_subtract_fusion
  199.3 0.6 gather_fusion.3
  200.0 0.1 copy.25
  200.1 0.6 select_select_fusion.6
  200.8 1.5 convolution_bitcast_fusion
  202.3 0.7 copy.33
  203.1 243.7 %all-reduce.6.cloned.1.call-done = f32[128,128]{0,1:T(8,128)} async-done(((f32[128,128]{0,1:T(8,128)}), f32[128,128]{0,1:T(8,128)}) %all-reduce.6.cloned.1.call-update) | async-done | bytes 65552 | tf_op jit(solution)/shard_map/psum | solution.py:69
  446.9 0.9 copy.26
  447.8 0.9 fusion.6
  448.6 11.7 %cholesky.44 = f32[128,128]{1,0:T(8,128)S(1)} custom-call(f32[128,128]{1,0:T(8,128)S(1)} %fusion.6), custom_call_target="Cholesky" | custom-call | tf_op jit(solution)/shard_map/jit(cholesky)/cholesky | solution.py:70
  460.4 0.6 compare_reduce_fusion.1
  461.0 0.7 fusion
  461.7 9.8 custom-call.6
  471.5 0.2 fusion.4
  471.7 0.7 gather_fusion.5
  472.3 0.1 copy.28
  472.4 0.6 select_select_fusion.5
  473.1 0.2 all-reduce.10.cloned.1.call-start
  473.3 3.4 reduce-scatter.9.cloned.1.call-done
  476.7 248.0 %all-reduce.8.cloned.1.call-done = f32[128,128]{0,1:T(8,128)} async-done(((f32[128,128]{0,1:T(8,128)}), f32[128,128]{0,1:T(8,128)}) %all-reduce.8.cloned.1.call-update) | async-done | bytes 65552 | tf_op jit(solution)/shard_map/psum | solution.py:62
  724.8 1.0 convolution_subtract_fusion
  725.8 0.6 gather_fusion.6
  726.5 0.1 copy.29
  726.6 0.6 select_select_fusion.4
  727.2 240.9 %all-reduce.10.cloned.1.call-done = f32[128,128]{0,1:T(8,128)} async-done(((f32[128,128]{0,1:T(8,128)}), f32[128,128]{0,1:T(8,128)}) %all-reduce.10.cloned.1.call-update) | async-done | bytes 65552 | tf_op jit(solution)/shard_map/psum | solution.py:69
  968.1 0.9 copy.30
  969.0 0.9 fusion.3
  969.9 11.7 %cholesky.55 = f32[128,128]{1,0:T(8,128)S(1)} custom-call(f32[128,128]{1,0:T(8,128)S(1)} %fusion.3), custom_call_target="Cholesky" | custom-call | tf_op jit(solution)/shard_map/jit(cholesky)/cholesky | solution.py:70
  981.6 0.6 compare_reduce_fusion
  982.3 0.7 fusion.1
  983.0 9.8 custom-call.7
  992.8 0.2 convolution_bitcast_fusion.2
  992.9 0.6 pad_maximum_fusion
  (30 shorter events, 0.4 us)
Async XLA Ops:
  6.5 3.5 copy-start
  6.5 156.3 %all-reduce.12.cloned.1.call-start = ((), (), s32[]{:S(2)}) async-start(), calls=%async_computation.7 | async-start | bytes 2097152 | tf_op jit(solution)/shard_map/psum | solution.py:43
  11.0 2.2 copy-start.2
  12.0 77.5 %copy-start.1 = (s32[2,128]{1,0:T(2,128)S(1)}, s32[2,128]{1,0:T(2,128)}, u32[]{:S(2)}) copy-start(s32[2,128]{1,0:T(2,128)} %param.13) | copy-start | bytes 3076
  13.2 185.3 %reduce-scatter.7.cloned.1.call-start = ((), (), s32[]{:S(2)}) async-start(), calls=%async_computation.5 | async-start | bytes 147456 | tf_op jit(solution)/shard_map/reduce_scatter | solution.py:51
  165.2 281.7 %all-reduce.6.cloned.1.call-start = ((), (), s32[]{:S(2)}) async-start(), calls=%async_computation.2 | async-start | bytes 131072 | tf_op jit(solution)/shard_map/psum | solution.py:69
  200.7 276.0 %reduce-scatter.9.cloned.1.call-start = ((), (), s32[]{:S(2)}) async-start(), calls=%async_computation.6 | async-start | bytes 147456 | tf_op jit(solution)/shard_map/reduce_scatter | solution.py:51
  203.1 521.7 %all-reduce.8.cloned.1.call-start = ((), (), s32[]{:S(2)}) async-start(), calls=%async_computation.3 | async-start | bytes 131072 | tf_op jit(solution)/shard_map/psum | solution.py:62
  473.1 495.0 %all-reduce.10.cloned.1.call-start = ((), (), s32[]{:S(2)}) async-start(), calls=%async_computation.4 | async-start | bytes 131072 | tf_op jit(solution)/shard_map/psum | solution.py:69
Sparse Core Ops, SparseCore 0:
  13.3 149.5 all-reduce.11
  165.4 33.0 reduce-scatter.6
  204.0 242.7 all-reduce.5
  449.2 27.4 reduce-scatter.8
  482.1 242.6 all-reduce.7
  730.2 237.9 all-reduce.9
where the time goes:
time: 1000 us
  waiting for transfers between devices  840 us (84%)
  blocking collectives  73.2 us (7%)
  other arithmetic  53.6 us (5%)
  local copies, waits for them, and re-layouts  15.6 us (2%)
  between operations  13.7 us (1%)
    psum x2, waiting for transfers between devices, shards(): block = lax.psum(pick_rows(current, chosen, share_first), ('rows', 'vecs'))  485 us
    psum x1, waiting for transfers between devices, shards(): lax.psum(pick_rows(stacked, chosen, share_first), ('rows', 'vecs'))  248 us
    all_gather x1, blocking collectives, shards(): every_point = lax.all_gather(coords, ('rows', 'vecs'), axis=1, tiled=True)  73.2 us
    psum x1, waiting for transfers between devices, shards(): lax.psum(pick_rows(old_vectors, chosen, block_first), 'rows')  70.1 us
    reduce_scatter x2, waiting for transfers between devices, shards(): lax.psum_scatter(residual_term(jnp.int32(0), share * lax.axis_size('vecs'...  36.7 us
    another operation x6, other arithmetic, shards(): factor = jnp.linalg.cholesky(block)  24.8 us
    another operation x4, other arithmetic, shards(): fresh = jax.scipy.linalg.solve_triangular(factor, current.T, lower=True).T  20.9 us
  transfers between devices with their start and end apart: 6, of which 6 were waited for; matrix products, arithmetic and copies ran while one was open for 3% of the time, Pallas kernels for 0%

commit v1 on v0

--- a/solution.py
+++ b/solution.py
@@ -66,7 +66,8 @@
                 precision=lax.Precision.HIGHEST,
                 preferred_element_type=jnp.float32,
             )
-        block = lax.psum(pick_rows(current, chosen, share_first), ("rows", "vecs"))
+        partial = lax.psum(pick_rows(current, chosen, share_first), "vecs")
+        block = lax.psum(partial, "rows")
         factor = jnp.linalg.cholesky(block)
         fresh = jax.scipy.linalg.solve_triangular(factor, current.T, lower=True).T
         new_panels.append(fresh)

time: 1000 us -> 930 us (0.930)
  waiting for transfers between devices: 840 us -> 765 us
    psum x2 -> x4, waiting for transfers between devices: 485 us -> 404 us  [the longest x2 281 us: shards(): block = lax.psum(partial, 'rows')]
  transfers between devices with their start and end apart: 6 -> 8, of which waited for: 6 -> 8; matrix products, arithmetic and copies ran while one was open for 3% -> 4% of each run, Pallas kernels for 0% -> 0%
where the time goes in v1:
time: 930 us; the launch traced here: 926 us
  waiting for transfers between devices  765 us (82%)
  blocking collectives  73.2 us (8%)
  other arithmetic  53.6 us (6%)
  local copies, waits for them, and re-layouts  15.6 us (2%)
  between operations  13.7 us (1%)
    psum x2, waiting for transfers between devices, shards(): block = lax.psum(partial, 'rows')  281 us
    psum x1, waiting for transfers between devices, shards(): lax.psum(pick_rows(stacked, chosen, share_first), ('rows', 'vecs'))  248 us
    psum x2, waiting for transfers between devices, shards(): partial = lax.psum(pick_rows(current, chosen, share_first), 'vecs')  123 us
    all_gather x1, blocking collectives, shards(): every_point = lax.all_gather(coords, ('rows', 'vecs'), axis=1, tiled=True)  73.2 us
    psum x1, waiting for transfers between devices, shards(): lax.psum(pick_rows(old_vectors, chosen, block_first), 'rows')  70.1 us
    reduce_scatter x2, waiting for transfers between devices, shards(): lax.psum_scatter(residual_term(jnp.int32(0), share * lax.axis_size('vecs'...  43.2 us
    another operation x6, other arithmetic, shards(): factor = jnp.linalg.cholesky(block)  24.8 us
    another operation x4, other arithmetic, shards(): fresh = jax.scipy.linalg.solve_triangular(factor, current.T, lower=True).T  20.9 us
  transfers between devices with their start and end apart: 8, of which 8 were waited for; matrix products, arithmetic and copies ran while one was open for 4% of the time, Pallas kernels for 0%

profile of v1, /device:TPU:1, one launch (start us, length us, event | category | flops | bytes accessed | tf_op | source)
XLA Modules:
  0.0 926.1 jit_solution(4646000098382469093)
XLA Ops:
  6.5 0.8 compare_select_fusion.1
  7.3 2.0 gather_fusion
  9.3 0.7 compare_and_fusion.7
  10.1 0.9 gather_fusion.4
  11.0 0.9 gather_fusion.2
  12.0 1.2 select_select_fusion
  13.2 73.2 %all-gather = f32[256,32,3]{1,2,0:T(4,128)S(1)} all-gather(f32[1,32,3]{1,2,0:T(4,128)S(1)} %bitcast.66), channel_id=1, replica_groups=mesh['rows'=32,'vecs'=8] {'rows','vecs'}, dimensions={0}, use_global_device_ids=true | all-gather | bytes 98688 | tf_op jit(solution)/shard_map/all_gather | solution.py:37
  86.5 3.0 copy.23
  89.5 2.9 gather_fusion.1
  92.4 0.1 select_bitcast_fusion
  92.5 0.3 slice_reduce_fusion.2
  92.8 70.1 %all-reduce.18.cloned.1.call-done = (bf16[128,2048]{1,0:T(8,128)(2,1)}, bf16[128,2048]{1,0:T(8,128)(2,1)}) async-done(((bf16[128,2048]{1,0:T(8,128)(2,1)}, bf16[128,2048]{1,0:T(8,128)(2,1)}), (bf16[128,2048]{1,0:T(8,128)(2,1)}, bf16[128,2048]{1,0:T(8,128)(2,1)})) %all-reduce.18.cloned.1.call-update) | async-done | bytes 1048592 | tf_op jit(solution)/shard_map/psum | solution.py:43
  162.9 1.5 convolution_bitcast_fusion.1
  164.4 0.7 copy.31
  165.3 33.3 %reduce-scatter.7.cloned.1.call-done = f32[32,128]{1,0:T(8,128)} async-done(((f32[256,128]{1,0:T(8,128)}), f32[32,128]{1,0:T(8,128)}) %reduce-scatter.7.cloned.1.call-update) | async-done | bytes 16400 | tf_op jit(solution)/shard_map/reduce_scatter | solution.py:51
  198.5 0.8 add_subtract_fusion
  199.3 0.6 gather_fusion.3
  200.0 0.1 copy.25
  200.1 0.6 select_select_fusion.6
  200.8 64.0 %all-reduce.8.cloned.1.call-done = f32[128,128]{0,1:T(8,128)} async-done(((f32[128,128]{0,1:T(8,128)}), f32[128,128]{0,1:T(8,128)}) %all-reduce.8.cloned.1.call-update) | async-done | bytes 65552 | tf_op jit(solution)/shard_map/psum | solution.py:69
  264.9 1.5 convolution_bitcast_fusion
  266.4 0.7 copy.33
  267.3 139.0 %all-reduce.10.cloned.1.call-done = f32[128,128]{0,1:T(8,128)} async-done(((f32[128,128]{0,1:T(8,128)}), f32[128,128]{0,1:T(8,128)}) %all-reduce.10.cloned.1.call-update) | async-done | bytes 65552 | tf_op jit(solution)/shard_map/psum | solution.py:70
  406.3 0.9 copy.26
  407.2 0.9 fusion.6
  408.1 11.7 %cholesky.44 = f32[128,128]{1,0:T(8,128)S(1)} custom-call(f32[128,128]{1,0:T(8,128)S(1)} %fusion.6), custom_call_target="Cholesky" | custom-call | tf_op jit(solution)/shard_map/jit(cholesky)/cholesky | solution.py:71
  419.8 0.6 compare_reduce_fusion.1
  420.5 0.7 fusion
  421.1 9.8 %custom-call.6 = f32[1,128,128]{1,2,0:T(8,128)S(1)} custom-call(f32[1,128,128]{2,1,0:T(8,128)S(1)} %fusion), custom_call_target="InvertDiagBlocksLowerTriangular" | custom-call | tf_op jit(solution)/shard_map/jit(_solve_triangular)/triangular_solve | solution.py:72
  431.0 0.2 fusion.4
  431.1 0.7 gather_fusion.5
  431.9 0.6 select_select_fusion.5
  432.6 9.9 %reduce-scatter.9.cloned.1.call-done = f32[32,128]{1,0:T(8,128)} async-done(((f32[256,128]{1,0:T(8,128)}), f32[32,128]{1,0:T(8,128)}) %reduce-scatter.9.cloned.1.call-update) | async-done | bytes 16400 | tf_op jit(solution)/shard_map/reduce_scatter | solution.py:51
  442.5 248.1 %all-reduce.12.cloned.1.call-done = f32[128,128]{0,1:T(8,128)} async-done(((f32[128,128]{0,1:T(8,128)}), f32[128,128]{0,1:T(8,128)}) %all-reduce.12.cloned.1.call-update) | async-done | bytes 65552 | tf_op jit(solution)/shard_map/psum | solution.py:62
  690.6 1.0 convolution_subtract_fusion
  691.6 0.6 gather_fusion.6
  692.4 0.6 select_select_fusion.4
  693.0 0.2 all-reduce.16.cloned.1.call-start
  693.2 59.0 %all-reduce.14.cloned.1.call-done = f32[128,128]{0,1:T(8,128)} async-done(((f32[128,128]{0,1:T(8,128)}), f32[128,128]{0,1:T(8,128)}) %all-reduce.14.cloned.1.call-update) | async-done | bytes 65552 | tf_op jit(solution)/shard_map/psum | solution.py:69
  752.2 141.6 %all-reduce.16.cloned.1.call-done = f32[128,128]{0,1:T(8,128)} async-done(((f32[128,128]{0,1:T(8,128)}), f32[128,128]{0,1:T(8,128)}) %all-reduce.16.cloned.1.call-update) | async-done | bytes 65552 | tf_op jit(solution)/shard_map/psum | solution.py:70
  893.8 0.9 copy.30
  894.7 0.9 fusion.3
  895.6 11.7 %cholesky.55 = f32[128,128]{1,0:T(8,128)S(1)} custom-call(f32[128,128]{1,0:T(8,128)S(1)} %fusion.3), custom_call_target="Cholesky" | custom-call | tf_op jit(solution)/shard_map/jit(cholesky)/cholesky | solution.py:71
  907.3 0.6 compare_reduce_fusion
  908.0 0.7 fusion.1
  908.6 9.8 %custom-call.7 = f32[1,128,128]{1,2,0:T(8,128)S(1)} custom-call(f32[1,128,128]{2,1,0:T(8,128)S(1)} %fusion.1), custom_call_target="InvertDiagBlocksLowerTriangular" | custom-call | tf_op jit(solution)/shard_map/jit(_solve_triangular)/triangular_solve | solution.py:72
  918.4 0.2 convolution_bitcast_fusion.2
  918.6 0.6 pad_maximum_fusion
  (36 shorter events, 0.7 us)
Async XLA Ops:
  6.5 3.5 copy-start
  6.5 156.3 %all-reduce.18.cloned.1.call-start = ((), (), s32[]{:S(2)}) async-start(), calls=%async_computation.9 | async-start | bytes 2097152 | tf_op jit(solution)/shard_map/psum | solution.py:43
  11.0 2.2 copy-start.2
  12.0 77.5 %copy-start.1 = (s32[2,128]{1,0:T(2,128)S(1)}, s32[2,128]{1,0:T(2,128)}, u32[]{:S(2)}) copy-start(s32[2,128]{1,0:T(2,128)} %param.13) | copy-start | bytes 3076
  13.2 185.3 %reduce-scatter.7.cloned.1.call-start = ((), (), s32[]{:S(2)}) async-start(), calls=%async_computation.7 | async-start | bytes 147456 | tf_op jit(solution)/shard_map/reduce_scatter | solution.py:51
  165.2 99.7 %all-reduce.8.cloned.1.call-start = ((), (), s32[]{:S(2)}) async-start(), calls=%async_computation.2 | async-start | bytes 131072 | tf_op jit(solution)/shard_map/psum | solution.py:69
  200.7 205.5 %all-reduce.10.cloned.1.call-start = ((), (), s32[]{:S(2)}) async-start(), calls=%async_computation.3 | async-start | bytes 131072 | tf_op jit(solution)/shard_map/psum | solution.py:70
  264.9 177.6 %reduce-scatter.9.cloned.1.call-start = ((), (), s32[]{:S(2)}) async-start(), calls=%async_computation.8 | async-start | bytes 147456 | tf_op jit(solution)/shard_map/reduce_scatter | solution.py:51
  267.2 423.4 %all-reduce.12.cloned.1.call-start = ((), (), s32[]{:S(2)}) async-start(), calls=%async_computation.4 | async-start | bytes 131072 | tf_op jit(solution)/shard_map/psum | solution.py:62
  432.5 319.7 %all-reduce.14.cloned.1.call-start = ((), (), s32[]{:S(2)}) async-start(), calls=%async_computation.5 | async-start | bytes 131072 | tf_op jit(solution)/shard_map/psum | solution.py:69
  693.0 200.8 %all-reduce.16.cloned.1.call-start = ((), (), s32[]{:S(2)}) async-start(), calls=%async_computation.6 | async-start | bytes 131072 | tf_op jit(solution)/shard_map/psum | solution.py:70
Sparse Core Ops, SparseCore 0:
  13.3 149.5 all-reduce.17
  165.4 33.0 reduce-scatter.6
  200.9 63.9 all-reduce.7
  268.1 138.0 all-reduce.9
  408.6 33.8 reduce-scatter.8
  447.9 242.6 all-reduce.11
  693.1 59.0 all-reduce.13
  755.6 138.0 all-reduce.15

commit v2 on v0

--- a/solution.py
+++ b/solution.py
@@ -5,6 +5,10 @@
 
 length_scale = 0.5
 noise_shift = 12.0
+
+
+def _bind_masks(raw):
+    return jnp.sum(lax.all_gather(raw, "rows"), axis=0)
 
 
 def matern(points, centers):
@@ -40,7 +44,7 @@
     for panel in range(panels):
         chosen = wanted[panel * width : (panel + 1) * width]
         old_pivot = (
-            lax.psum(pick_rows(old_vectors, chosen, block_first), "rows")
+            _bind_masks(pick_rows(old_vectors, chosen, block_first))
             .astype(jnp.float32)
             .astype(jnp.bfloat16)
         )

time: 1000 us -> 1130 us (1.13)
  waiting for transfers between devices: 840 us -> 949 us
  other arithmetic: 53.6 us -> 72 us
    all_gather x0 -> x2, waiting for transfers between devices: none -> 189 us  [_bind_masks(): return jnp.sum(lax.all_gather(raw, 'rows'), axis=0)]
    psum x1 -> x0, waiting for transfers between devices: 70.1 us -> none  [shards(): lax.psum(pick_rows(old_vectors, chosen, block_first), 'rows')]
    reduce_sum x0 -> x2, other arithmetic: none -> 17.7 us  [_bind_masks(): return jnp.sum(lax.all_gather(raw, 'rows'), axis=0)]
  transfers between devices with their start and end apart: 6 -> 7, of which waited for: 6 -> 7; matrix products, arithmetic and copies ran while one was open for 3% -> 5% of each run, Pallas kernels for 0% -> 0%
where the time goes in v2:
time: 1130 us
  waiting for transfers between devices  949 us (84%)
  blocking collectives  74.5 us (7%)
  other arithmetic  72 us (6%)
  local copies, waits for them, and re-layouts  15.7 us (1%)
  between operations  13.7 us (1%)
    psum x2, waiting for transfers between devices, shards(): block = lax.psum(pick_rows(current, chosen, share_first), ('rows', 'vecs'))  485 us
    psum x1, waiting for transfers between devices, shards(): lax.psum(pick_rows(stacked, chosen, share_first), ('rows', 'vecs'))  248 us
    all_gather x2, waiting for transfers between devices, _bind_masks(): return jnp.sum(lax.all_gather(raw, 'rows'), axis=0)  189 us
    all_gather x1, blocking collectives, shards(): every_point = lax.all_gather(coords, ('rows', 'vecs'), axis=1, tiled=True)  74.5 us
    reduce_scatter x2, waiting for transfers between devices, shards(): lax.psum_scatter(residual_term(jnp.int32(0), share * lax.axis_size('vecs'...  26 us
    another operation x6, other arithmetic, shards(): factor = jnp.linalg.cholesky(block)  24.8 us
  transfers between devices with their start and end apart: 7, of which 7 were waited for; matrix products, arithmetic and copies ran while one was open for 5% of the time, Pallas kernels for 0%

profile of v2, /device:TPU:1, one launch (start us, length us, event | category | flops | bytes accessed | tf_op | source)
XLA Modules:
  0.0 1127.6 jit_solution(4638145909487737025)
XLA Ops:
  6.5 0.8 compare_select_fusion.1
  7.3 2.0 gather_fusion
  9.3 0.7 compare_and_fusion.7
  10.0 0.9 gather_fusion.2
  11.0 1.0 select_select_fusion.1
  12.0 0.9 gather_fusion.4
  13.0 1.0 select_select_fusion
  14.0 74.5 %all-gather.2 = f32[256,32,3]{1,2,0:T(4,128)S(1)} all-gather(f32[1,32,3]{1,2,0:T(4,128)} %bitcast.70), channel_id=1, replica_groups=mesh['rows'=32,'vecs'=8] {'rows','vecs'}, dimensions={0}, use_global_device_ids=true | all-gather | bytes 98688 | tf_op jit(solution)/shard_map/all_gather | solution.py:41
  88.5 3.1 copy.23
  91.6 2.9 gather_fusion.1
  94.6 0.3 slice_reduce_fusion.2
  94.9 60.0 %all-gather.6.cloned.1.call-done = bf16[4096,2048]{1,0:T(8,128)(2,1)} async-done(((bf16[128,2048]{1,0:T(8,128)(2,1)}), bf16[4096,2048]{1,0:T(8,128)(2,1)}) %all-gather.6.cloned.1.call-update) | async-done | bytes 16777232 | tf_op jit(solution)/shard_map/all_gather | solution.py:11
  155.0 8.9 reduce_sum.24
  163.8 0.5 convolution_bitcast_fusion.1
  164.3 0.7 copy.31
  165.2 129.2 %all-gather.8.cloned.1.call-done = bf16[4096,2048]{1,0:T(8,128)(2,1)} async-done(((bf16[128,2048]{1,0:T(8,128)(2,1)}), bf16[4096,2048]{1,0:T(8,128)(2,1)}) %all-gather.8.cloned.1.call-update) | async-done | bytes 16777232 | tf_op jit(solution)/shard_map/all_gather | solution.py:11
  294.4 8.9 reduce_sum.25
  303.2 22.6 %reduce-scatter.7.cloned.1.call-done = f32[32,128]{1,0:T(8,128)} async-done(((f32[256,128]{1,0:T(8,128)}), f32[32,128]{1,0:T(8,128)}) %reduce-scatter.7.cloned.1.call-update) | async-done | bytes 16400 | tf_op jit(solution)/shard_map/reduce_scatter | solution.py:55
  325.9 0.8 add_subtract_fusion
  326.7 0.6 gather_fusion.3
  327.4 0.6 select_select_fusion.6
  328.1 0.5 convolution_bitcast_fusion
  328.6 0.7 copy.33
  329.4 0.2 all-reduce.6.cloned.1.call-start
  329.6 244.4 %all-reduce.4.cloned.1.call-done = f32[128,128]{0,1:T(8,128)} async-done(((f32[128,128]{0,1:T(8,128)}), f32[128,128]{0,1:T(8,128)}) %all-reduce.4.cloned.1.call-update) | async-done | bytes 65552 | tf_op jit(solution)/shard_map/psum | solution.py:73
  574.0 0.9 copy.26
  574.9 0.9 fusion.6
  575.8 11.7 %cholesky.44 = f32[128,128]{1,0:T(8,128)S(1)} custom-call(f32[128,128]{1,0:T(8,128)S(1)} %fusion.6), custom_call_target="Cholesky" | custom-call | tf_op jit(solution)/shard_map/jit(cholesky)/cholesky | solution.py:74
  587.5 0.6 compare_reduce_fusion.1
  588.1 0.7 fusion
  588.8 9.8 custom-call.6
  598.6 0.2 fusion.4
  598.8 0.7 gather_fusion.5
  599.5 0.6 select_select_fusion.5
  600.2 0.3 all-reduce.8.cloned.1.call-start
  600.5 3.4 reduce-scatter.9.cloned.1.call-done
  603.8 248.1 %all-reduce.6.cloned.1.call-done = f32[128,128]{0,1:T(8,128)} async-done(((f32[128,128]{0,1:T(8,128)}), f32[128,128]{0,1:T(8,128)}) %all-reduce.6.cloned.1.call-update) | async-done | bytes 65552 | tf_op jit(solution)/shard_map/psum | solution.py:66
  851.9 1.0 convolution_subtract_fusion
  852.9 0.6 gather_fusion.6
  853.7 0.6 select_select_fusion.4
  854.3 241.0 %all-reduce.8.cloned.1.call-done = f32[128,128]{0,1:T(8,128)} async-done(((f32[128,128]{0,1:T(8,128)}), f32[128,128]{0,1:T(8,128)}) %all-reduce.8.cloned.1.call-update) | async-done | bytes 65552 | tf_op jit(solution)/shard_map/psum | solution.py:73
  1095.3 0.9 copy.30
  1096.2 0.9 fusion.3
  1097.1 11.7 %cholesky.55 = f32[128,128]{1,0:T(8,128)S(1)} custom-call(f32[128,128]{1,0:T(8,128)S(1)} %fusion.3), custom_call_target="Cholesky" | custom-call | tf_op jit(solution)/shard_map/jit(cholesky)/cholesky | solution.py:74
  1108.8 0.6 compare_reduce_fusion
  1109.5 0.7 fusion.1
  1110.1 9.8 custom-call.7
  1120.1 0.6 pad_maximum_fusion
  (36 shorter events, 1.0 us)
Async XLA Ops:
  6.5 3.5 copy-start
  6.5 85.0 %copy-start.1 = (s32[2,128]{1,0:T(2,128)S(1)}, s32[2,128]{1,0:T(2,128)}, u32[]{:S(2)}) copy-start(s32[2,128]{1,0:T(2,128)} %param.13) | copy-start | bytes 3076
  6.5 148.4 %all-gather.6.cloned.1.call-start = ((), (), s32[]{:S(2)}) async-start(), calls=%async_computation.5 | async-start | bytes 17301504 | tf_op jit(solution)/shard_map/all_gather | solution.py:11
  11.0 154.2 %copy-start.2 = (f32[3,32]{1,0:T(4,128)S(1)}, f32[3,32]{1,0:T(4,128)}, u32[]{:S(2)}) copy-start(f32[3,32]{1,0:T(4,128)} %param.11) | copy-start | bytes 1156
  12.0 282.4 %all-gather.8.cloned.1.call-start = ((), (), s32[]{:S(2)}) async-start(), calls=%async_computation.6 | async-start | bytes 17301504 | tf_op jit(solution)/shard_map/all_gather | solution.py:11
  14.0 311.9 %reduce-scatter.7.cloned.1.call-start = ((), (), s32[]{:S(2)}) async-start(), calls=%async_computation.7 | async-start | bytes 147456 | tf_op jit(solution)/shard_map/reduce_scatter | solution.py:55
  165.1 408.9 %all-reduce.4.cloned.1.call-start = ((), (), s32[]{:S(2)}) async-start(), calls=%async_computation.2 | async-start | bytes 131072 | tf_op jit(solution)/shard_map/psum | solution.py:73
  328.1 275.8 %reduce-scatter.9.cloned.1.call-start = ((), (), s32[]{:S(2)}) async-start(), calls=%async_computation.8 | async-start | bytes 147456 | tf_op jit(solution)/shard_map/reduce_scatter | solution.py:55
  329.4 522.6 %all-reduce.6.cloned.1.call-start = ((), (), s32[]{:S(2)}) async-start(), calls=%async_computation.3 | async-start | bytes 131072 | tf_op jit(solution)/shard_map/psum | solution.py:66
  600.2 495.1 %all-reduce.8.cloned.1.call-start = ((), (), s32[]{:S(2)}) async-start(), calls=%async_computation.4 | async-start | bytes 131072 | tf_op jit(solution)/shard_map/psum | solution.py:73
Sparse Core Ops, SparseCore 0:
  12.1 142.8 all-gather.5
  157.6 136.7 all-gather.7
  296.9 28.9 reduce-scatter.6
  331.2 242.7 all-reduce.3
  576.3 27.4 reduce-scatter.8
  609.2 242.6 all-reduce.5
  857.4 237.8 all-reduce.7
